TPU v7x, 32 devices: a whole 2x2x4 slice. The times are simulated.
32 devices in a mesh: abl: 2 (over y), head: 4 (over x, core), ctx: 4 (over z).
Axes of the slice: x: 2, y: 2, z: 4, core: 2. Of those that a mesh axis runs over, the one named last changes fastest.
Arguments:
- queries: bfloat16 [1024, 6144], P(('abl', 'head', 'ctx')), parts along dimension 0, may hold values from -30 to 30
- keys: bfloat16 [16384, 6144], P(('abl', 'ctx'), 'head'), parts along dimension 0, may hold values from -6 to 6
- values: bfloat16 [16384, 6144], P(('abl', 'ctx'), 'head'), parts along dimension 0, may hold values from -6 to 6
- kept_rows: int32 [128], P(('abl', 'ctx')), parts along dimension 0, may hold values from 0 to 1, as said below
- out_weight: bfloat16 [6144, 6144], P('head'), may hold values from -6 to 6
Outputs:
- projected: bfloat16 [1024, 6144], P(('abl', 'head', 'ctx')), parts along dimension 0
There are 2 independent parts, one for each index of `abl`. A program takes and returns all parts, laid end to end along the dimension named above; an argument that names none is the same for every part. Nothing has to cross between parts.
Inputs may be any that keep to these rules, and one draw needn't show every extreme that they name: `kept_rows`: in every part the first row of each block of 16 consecutive rows is kept.
All inputs are finite; a program needn't handle non-finite values.
Results may differ from a plain program's by a relative error of at most 0.028.
Values may be sent and summed in bfloat16 or wider, within the bound.
No kernel may reach another device: no remote copies, remote signals or barrier semaphores. Data moves between devices by JAX's collectives and lax.ppermute only.
A program may use at most 128 MiB of HBM per device.

v0:
```python
import math
import jax
import jax.numpy as jnp
from jax import lax
from jax.sharding import PartitionSpec as P

HD = 128


def shards(queries, keys, values, kept_rows, out_weight):
    score_scale = 1.0 / math.sqrt(HD)
    local_heads = keys.shape[1] // HD
    key_count = keys.shape[0]
    key_heads = keys.reshape(key_count, local_heads, HD)
    value_heads = values.reshape(key_count, local_heads, HD)
    visible = jnp.repeat(kept_rows, 128) > 0
    query_block = lax.all_to_all(queries, "head", split_axis=1, concat_axis=0, tiled=True)
    all_queries = lax.all_gather(query_block, "ctx", axis=0, tiled=True)
    row_count = all_queries.shape[0]
    zeros_sum = jnp.zeros((row_count, local_heads * HD), jnp.float32)
    lowest = jnp.full((local_heads, row_count), -1e30, jnp.float32)
    summed = zeros_sum
    row_count = all_queries.shape[0]
    shaped = all_queries.reshape(row_count, local_heads, HD)
    scores = (
        jnp.einsum("qhd,khd->hqk", shaped, key_heads, preferred_element_type=jnp.float32)
        * score_scale
    )
    scores = jnp.where(visible[None, None, :], scores, -jnp.inf)
    highest = jnp.maximum(lowest, jnp.max(scores, axis=-1))
    rescale = jnp.exp(lowest - highest)
    softened = jnp.exp(scores - highest[..., None])
    normal_sum = jnp.sum(softened, axis=-1)
    mixed = jnp.einsum(
        "hqk,khd->qhd",
        softened.astype(jnp.bfloat16),
        value_heads,
        preferred_element_type=jnp.float32,
    )
    summed = summed * jnp.repeat(rescale.T, HD, axis=1) + mixed.reshape(row_count, local_heads * HD)
    summed, running, normal_sum = (summed, highest, normal_sum)
    highest = lax.pmax(running, "ctx")
    rescale = jnp.exp(running - highest)
    summed = summed * jnp.repeat(rescale.T, HD, axis=1)
    normal_sum = normal_sum * rescale
    summed, normal_sum = (
        lax.psum_scatter(
            summed.astype(jnp.bfloat16), "ctx", scatter_dimension=0, tiled=True
        ).astype(jnp.float32),
        lax.psum_scatter(
            normal_sum.astype(jnp.bfloat16), "ctx", scatter_dimension=1, tiled=True
        ).astype(jnp.float32),
    )
    attended = (summed / jnp.repeat(normal_sum.T, HD, axis=1)).astype(jnp.bfloat16)
    return lax.psum_scatter(
        jnp.dot(attended, out_weight, preferred_element_type=jnp.float32).astype(jnp.bfloat16),
        "head",
        scatter_dimension=0,
        tiled=True,
    )


def solution(mesh):
    placed = (
        P(("abl", "head", "ctx"), None),
        P(("abl", "ctx"), "head"),
        P(("abl", "ctx"), "head"),
        P(("abl", "ctx")),
        P("head", None),
    )
    return jax.shard_map(
        shards,
        mesh=mesh,
        in_specs=placed,
        out_specs=P(("abl", "head", "ctx"), None),
        check_vma=False,
    )
```

profile of v0, /device:TPU:0, one launch (start us, length us, event | category | flops | bytes accessed | tf_op | source)
XLA Modules:
  0.0 223.1 jit_solution(14071060724346164999)
XLA Ops:
  6.5 1.0 copy.33
  7.6 11.6 %all_to_all.19 = bf16[32,4,1536]{2,0,1:T(8,128)(2,1)} all-to-all(bf16[32,4,1536]{2,0,1:T(8,128)(2,1)S(1)} %bitcast.42), channel_id=1, replica_groups=mesh['abl'=2,'head'=4,'ctx'=4] {'head'}, dimensions={1} | all-to-all | bytes 786432 | tf_op jit(solution)/shard_map/all_to_all | solution.py:17
  19.1 0.0 all-gather.2.cloned.1.call-update
  19.2 0.0 reduce-scatter.12.cloned.1.call-start
  19.2 8.8 %copy.21 = bf16[2048,1536]{0,1:T(8,128)(2,1)} copy(bf16[2048,1536]{1,0:T(8,128)(2,1)} %param.6) | data formatting | bytes 12582912 | tf_op args[1]
  28.0 8.8 %copy.24 = bf16[2048,1536]{0,1:T(8,128)(2,1)} copy(bf16[2048,1536]{1,0:T(8,128)(2,1)} %param.7) | data formatting | bytes 12582912 | tf_op args[2]
  36.7 0.1 broadcast_bitcast_fusion
  36.8 20.3 %all-gather.2.cloned.1.call-done = bf16[512,1536]{1,0:T(8,128)(2,1)} async-done(((bf16[128,1536]{1,0:T(8,128)(2,1)}), bf16[512,1536]{1,0:T(8,128)(2,1)}) %all-gather.2.cloned.1.call-update) | async-done | bytes 1572880 | tf_op jit(solution)/shard_map/all_gather | solution.py:18
  57.1 1.7 copy.20
  58.8 22.6 %fusion = (f32[12,512]{1,0:T(8,128)S(1)}, f32[12,512,2048]{2,1,0:T(8,128)}) fusion(pred[2048]{0:T(1024)(128)(4,1)S(1)} %broadcast_bitcast_fusion, bf16[512,12,128]{0,2,1:T(8,128)(2,1)S(1)} %bitcast.38, bf16[2048,12,128]{0,2,1:T(8,128)(2,1)} %bitcast.37), kind=kOutput, calls=%fused_computation.2 | convolution fusion | flops 3258968064 | bytes 58222592 | tf_op jit(solution)/shard_map/qhd,khd->hqk/dot_general | solution.py:26
  81.4 16.9 %pmax.7 = f32[12,512]{1,0:T(8,128)S(1)} all-reduce(f32[12,512]{1,0:T(8,128)S(1)} %broadcast_maximum_fusion), channel_id=1, replica_groups=mesh['abl'=2,'head'=4,'ctx'=4] {'ctx'}, use_global_device_ids=true, to_apply=%region_1.2 | all-reduce | flops 6144 | bytes 49152 | tf_op jit(solution)/shard_map/pmax | solution.py:42
  98.4 21.1 %fusion.1 = f32[12,512]{1,0:T(8,128)S(1)} fusion(f32[12,512,2048]{2,1,0:T(8,128)} %get-tuple-element.9, f32[12,512]{1,0:T(8,128)S(1)} %broadcast_maximum_fusion, pred[2048]{0:T(1024)(128)(4,1)S(1)} %broadcast_bitcast_fusion), kind=kLoop, calls=%fused_computation.3 | loop fusion | flops 50325504 | bytes 50382848 | tf_op jit(solution)/shard_map/reduce_sum | solution.py:33
  119.5 0.8 copy.29
  120.3 0.0 reduce-scatter.10.cloned.1.call-start
  120.4 22.0 %fusion.7 = bf16[512,12,128]{0,2,1:T(8,128)(2,1)S(1)} fusion(bf16[2048,12,128]{0,2,1:T(8,128)(2,1)} %bitcast.39, f32[12,512,2048]{2,1,0:T(8,128)} %get-tuple-element.9, f32[12,512]{1,0:T(8,128)S(1)} %broadcast_maximum_fusion, pred[2048]{0:T(1024)(128)(4,1)S(1)} %broadcast_bitcast_fusion, f32[512,12]{0,1:T(8,128)S(1)} %get-tuple-element.6, ...), kind=kOutput, calls=%fused_computation.10 | convolution fusion | flops 3273916416 | bytes 58271744 | tf_op jit(solution)/shard_map/hqk,khd->qhd/dot_general | solution.py:34
  142.4 1.6 copy.27
  144.0 0.2 reduce-scatter.8.cloned.1.call-start
  144.2 0.0 reduce-scatter.12.cloned.1.call-done
  144.3 0.8 copy.30
  145.1 32.7 %reduce-scatter.10.cloned.1.call-done = bf16[128,1536]{1,0:T(8,128)(2,1)} async-done(((bf16[512,1536]{1,0:T(8,128)(2,1)}), bf16[128,1536]{1,0:T(8,128)(2,1)}) %reduce-scatter.10.cloned.1.call-update) | async-done | bytes 393232
  177.7 1.2 copy.28
  179.0 0.1 fusion.10
  179.1 10.2 %convolution_convert_fusion = bf16[128,6144]{1,0:T(8,128)(2,1)} fusion(bf16[128,1536]{0,1:T(8,128)(2,1)S(1)} %fusion.10, bf16[1536,6144]{1,0:T(8,128)(2,1)} %param.9), kind=kOutput, calls=%fused_computation.7 | convolution fusion | flops 2416705536 | bytes 20840448 | tf_op jit(solution)/shard_map/dot_general | solution.py:56
  189.3 27.3 %reduce-scatter.8.cloned.1.call-done = bf16[32,6144]{1,0:T(8,128)(2,1)} async-done(((bf16[128,6144]{1,0:T(8,128)(2,1)}), bf16[32,6144]{1,0:T(8,128)(2,1)}) %reduce-scatter.8.cloned.1.call-update) | async-done | bytes 393232 | tf_op jit(solution)/shard_map/reduce_scatter | solution.py:55
  (10 shorter events, 0.1 us)
Async XLA Ops:
  6.5 30.2 %copy-start = (s32[16]{0:T(128)S(1)}, s32[16]{0:T(128)}, u32[]{:S(2)}) copy-start(s32[16]{0:T(128)} %param.8) | copy-start | bytes 196
  6.5 50.6 %all-gather.2.cloned.1.call-start = ((), (), s32[]{:S(2)}) async-start(), calls=%async_computation.4 | async-start | bytes 1966080 | tf_op jit(solution)/shard_map/all_gather | solution.py:18
  19.2 125.1 %reduce-scatter.12.cloned.1.call-start = ((), (), s32[]{:S(2)}) async-start(), calls=%async_computation.7 | async-start | bytes 163840
  120.3 57.4 %reduce-scatter.10.cloned.1.call-start = ((), (), s32[]{:S(2)}) async-start(), calls=%async_computation.6 | async-start | bytes 1966080
  144.0 72.6 %reduce-scatter.8.cloned.1.call-start = ((), (), s32[]{:S(2)}) async-start(), calls=%async_computation.5 | async-start | bytes 1966080 | tf_op jit(solution)/shard_map/reduce_scatter | solution.py:55
Sparse Core Ops, SparseCore 0:
  19.3 37.8 all-gather.1
  120.4 17.4 reduce-scatter.11
  144.1 33.5 reduce-scatter.9
  189.4 27.1 reduce-scatter.7
where the time goes:
time: 224 us; the launch traced here: 223 us
  waiting for transfers between devices  80.4 us (36%)
  matrix products  54.9 us (25%)
  blocking collectives  28.5 us (13%)
  local copies, waits for them, and re-layouts  24.7 us (11%)
  other arithmetic  21.2 us (9%)
  between operations  13.2 us (6%)
    unnamed x6, waiting for transfers between devices  32.7 us
    reduce_scatter x1, waiting for transfers between devices, shards(): lax.psum_scatter(jnp.dot(attended, out_weight, preferred_element_type=jnp...  27.3 us
    dot_general x1, matrix products, shards(): jnp.einsum('qhd,khd->hqk', shaped, key_heads, preferred_element_type=jnp....  22.6 us
    dot_general x1, matrix products, shards(): jnp.einsum('hqk,khd->qhd', softened.astype(jnp.bfloat16), value_heads, pr...  22 us
    unnamed x8, local copies, waits for them, and re-layouts  21.9 us
    reduce_sum x1, other arithmetic, shards(): normal_sum = jnp.sum(softened, axis=-1)  21.1 us
    all_gather x1, waiting for transfers between devices, shards(): all_queries = lax.all_gather(query_block, 'ctx', axis=0, tiled=True)  20.3 us
    pmax x1, blocking collectives, shards(): highest = lax.pmax(running, 'ctx')  16.9 us
  transfers between devices with their start and end apart: 4, of which 3 were waited for; matrix products, arithmetic and copies ran while one was open for 19% of the time, Pallas kernels for 0%

commit v1 on v0

--- a/solution.py
+++ b/solution.py
@@ -14,7 +14,10 @@
     key_heads = keys.reshape(key_count, local_heads, HD)
     value_heads = values.reshape(key_count, local_heads, HD)
     visible = jnp.repeat(kept_rows, 128) > 0
-    query_block = lax.all_to_all(queries, "head", split_axis=1, concat_axis=0, tiled=True)
+    query_block = jnp.concatenate(
+        lax.all_to_all(jnp.stack(jnp.split(queries, lax.axis_size("head"), axis=1)), "head", 0, 0),
+        axis=0,
+    )
     all_queries = lax.all_gather(query_block, "ctx", axis=0, tiled=True)
     row_count = all_queries.shape[0]
     zeros_sum = jnp.zeros((row_count, local_heads * HD), jnp.float32)

time: 224 us -> 224 us (level)
  no operation moved by 1% of the time
where the time goes in v1:
time: 224 us; the launch traced here: 223 us
  waiting for transfers between devices  80.4 us (36%)
  matrix products  54.9 us (25%)
  blocking collectives  28.5 us (13%)
  local copies, waits for them, and re-layouts  24.8 us (11%)
  other arithmetic  21.3 us (10%)
  between operations  13.2 us (6%)
    unnamed x6, waiting for transfers between devices  32.7 us
    reduce_scatter x1, waiting for transfers between devices, shards(): lax.psum_scatter(jnp.dot(attended, out_weight, preferred_element_type=jnp...  27.3 us
    dot_general x1, matrix products, shards(): jnp.einsum('qhd,khd->hqk', shaped, key_heads, preferred_element_type=jnp....  22.6 us
    dot_general x1, matrix products, shards(): jnp.einsum('hqk,khd->qhd', softened.astype(jnp.bfloat16), value_heads, pr...  22 us
    unnamed x8, local copies, waits for them, and re-layouts  21.9 us
    reduce_sum x1, other arithmetic, shards(): normal_sum = jnp.sum(softened, axis=-1)  21.1 us
    all_gather x1, waiting for transfers between devices, shards(): all_queries = lax.all_gather(query_block, 'ctx', axis=0, tiled=True)  20.3 us
    pmax x1, blocking collectives, shards(): highest = lax.pmax(running, 'ctx')  16.9 us
  transfers between devices with their start and end apart: 4, of which 3 were waited for; matrix products, arithmetic and copies ran while one was open for 19% of the time, Pallas kernels for 0%

profile of v1, /device:TPU:0, one launch (start us, length us, event | category | flops | bytes accessed | tf_op | source)
XLA Modules:
  0.0 223.2 jit_solution(15220883077394763500)
XLA Ops:
  6.5 1.1 slice_bitcast_fusion.3
  7.6 0.1 pad_maximum_fusion
  7.7 11.6 %all_to_all.5 = bf16[4,32,1536]{2,1,0:T(8,128)(2,1)} all-to-all(bf16[4,32,1536]{2,1,0:T(8,128)(2,1)S(1)} %pad_maximum_fusion), channel_id=1, replica_groups=mesh['abl'=2,'head'=4,'ctx'=4] {'head'}, dimensions={0} | all-to-all | bytes 786432 | tf_op jit(solution)/shard_map/all_to_all | solution.py:18
  19.3 0.0 reduce-scatter.12.cloned.1.call-start
  19.3 8.8 %copy.19 = bf16[2048,1536]{0,1:T(8,128)(2,1)} copy(bf16[2048,1536]{1,0:T(8,128)(2,1)} %param.6) | data formatting | bytes 12582912 | tf_op args[1]
  28.1 8.8 %copy.22 = bf16[2048,1536]{0,1:T(8,128)(2,1)} copy(bf16[2048,1536]{1,0:T(8,128)(2,1)} %param.7) | data formatting | bytes 12582912 | tf_op args[2]
  36.8 0.1 broadcast_bitcast_fusion
  36.9 20.3 %all-gather.2.cloned.1.call-done = bf16[512,1536]{1,0:T(8,128)(2,1)} async-done(((bf16[128,1536]{1,0:T(8,128)(2,1)}), bf16[512,1536]{1,0:T(8,128)(2,1)}) %all-gather.2.cloned.1.call-update) | async-done | bytes 1572880 | tf_op jit(solution)/shard_map/all_gather | solution.py:21
  57.2 1.7 copy.18
  59.0 22.6 %fusion = (f32[12,512]{1,0:T(8,128)S(1)}, f32[12,512,2048]{2,1,0:T(8,128)}) fusion(pred[2048]{0:T(1024)(128)(4,1)S(1)} %broadcast_bitcast_fusion, bf16[512,12,128]{0,2,1:T(8,128)(2,1)S(1)} %bitcast.40, bf16[2048,12,128]{0,2,1:T(8,128)(2,1)} %bitcast.39), kind=kOutput, calls=%fused_computation.2 | convolution fusion | flops 3258968064 | bytes 58222592 | tf_op jit(solution)/shard_map/qhd,khd->hqk/dot_general | solution.py:29
  81.5 16.9 %pmax.7 = f32[12,512]{1,0:T(8,128)S(1)} all-reduce(f32[12,512]{1,0:T(8,128)S(1)} %broadcast_maximum_fusion), channel_id=1, replica_groups=mesh['abl'=2,'head'=4,'ctx'=4] {'ctx'}, use_global_device_ids=true, to_apply=%region_1.2 | all-reduce | flops 6144 | bytes 49152 | tf_op jit(solution)/shard_map/pmax | solution.py:45
  98.5 21.1 %fusion.1 = f32[12,512]{1,0:T(8,128)S(1)} fusion(f32[12,512,2048]{2,1,0:T(8,128)} %get-tuple-element.13, f32[12,512]{1,0:T(8,128)S(1)} %broadcast_maximum_fusion, pred[2048]{0:T(1024)(128)(4,1)S(1)} %broadcast_bitcast_fusion), kind=kLoop, calls=%fused_computation.3 | loop fusion | flops 50325504 | bytes 50382848 | tf_op jit(solution)/shard_map/reduce_sum | solution.py:36
  119.6 0.8 copy.27
  120.4 0.0 reduce-scatter.10.cloned.1.call-start
  120.5 22.0 %fusion.7 = bf16[512,12,128]{0,2,1:T(8,128)(2,1)S(1)} fusion(bf16[2048,12,128]{0,2,1:T(8,128)(2,1)} %bitcast.41, f32[12,512,2048]{2,1,0:T(8,128)} %get-tuple-element.13, f32[12,512]{1,0:T(8,128)S(1)} %broadcast_maximum_fusion, pred[2048]{0:T(1024)(128)(4,1)S(1)} %broadcast_bitcast_fusion, f32[512,12]{0,1:T(8,128)S(1)} %get-tuple-element.10, ...), kind=kOutput, calls=%fused_computation.10 | convolution fusion | flops 3273916416 | bytes 58271744 | tf_op jit(solution)/shard_map/hqk,khd->qhd/dot_general | solution.py:37
  142.5 1.6 copy.25
  144.1 0.2 reduce-scatter.8.cloned.1.call-start
  144.3 0.0 reduce-scatter.12.cloned.1.call-done
  144.4 0.8 copy.28
  145.2 32.7 %reduce-scatter.10.cloned.1.call-done = bf16[128,1536]{1,0:T(8,128)(2,1)} async-done(((bf16[512,1536]{1,0:T(8,128)(2,1)}), bf16[128,1536]{1,0:T(8,128)(2,1)}) %reduce-scatter.10.cloned.1.call-update) | async-done | bytes 393232
  177.8 1.2 copy.26
  179.1 0.1 fusion.10
  179.2 10.2 %convolution_convert_fusion = bf16[128,6144]{1,0:T(8,128)(2,1)} fusion(bf16[128,1536]{0,1:T(8,128)(2,1)S(1)} %fusion.10, bf16[1536,6144]{1,0:T(8,128)(2,1)} %param.9), kind=kOutput, calls=%fused_computation.7 | convolution fusion | flops 2416705536 | bytes 20840448 | tf_op jit(solution)/shard_map/dot_general | solution.py:59
  189.4 27.3 %reduce-scatter.8.cloned.1.call-done = bf16[32,6144]{1,0:T(8,128)(2,1)} async-done(((bf16[128,6144]{1,0:T(8,128)(2,1)}), bf16[32,6144]{1,0:T(8,128)(2,1)}) %reduce-scatter.8.cloned.1.call-update) | async-done | bytes 393232 | tf_op jit(solution)/shard_map/reduce_scatter | solution.py:58
  (11 shorter events, 0.1 us)
Async XLA Ops:
  6.5 30.3 %copy-start = (s32[16]{0:T(128)S(1)}, s32[16]{0:T(128)}, u32[]{:S(2)}) copy-start(s32[16]{0:T(128)} %param.8) | copy-start | bytes 196
  6.5 50.7 %all-gather.2.cloned.1.call-start = ((), (), s32[]{:S(2)}) async-start(), calls=%async_computation.4 | async-start | bytes 1966080 | tf_op jit(solution)/shard_map/all_gather | solution.py:21
  19.3 125.1 %reduce-scatter.12.cloned.1.call-start = ((), (), s32[]{:S(2)}) async-start(), calls=%async_computation.7 | async-start | bytes 163840
  120.4 57.4 %reduce-scatter.10.cloned.1.call-start = ((), (), s32[]{:S(2)}) async-start(), calls=%async_computation.6 | async-start | bytes 1966080
  144.1 72.6 %reduce-scatter.8.cloned.1.call-start = ((), (), s32[]{:S(2)}) async-start(), calls=%async_computation.5 | async-start | bytes 1966080 | tf_op jit(solution)/shard_map/reduce_scatter | solution.py:58
Sparse Core Ops, SparseCore 0:
  19.4 37.8 all-gather.1
  120.5 17.4 reduce-scatter.11
  144.2 33.5 reduce-scatter.9
  189.5 27.1 reduce-scatter.7
